TPU v7x, 512 devices: a whole 4x8x8 slice. The times are simulated.
512 devices in a mesh: dp: 64 (over y, x, core), tensor: 8 (over z).
Axes of the slice: x: 4, y: 8, z: 8, core: 2. Of those that a mesh axis runs over, the one named last changes fastest.
Arguments:
- hidden_act: bfloat16 [32768, 1408], P('dp', 'tensor'), may hold values from -6 to 6
- cotangent: bfloat16 [32768, 2048], P('dp', 'tensor'), may hold values from -4 to 4
- down_table: bfloat16 [1408, 64, 2048], P('tensor', 'dp'), may hold values from -0.15625 to 0.15625
- expert_ids: int32 [128, 4], P('dp'), may hold values from 0 to 31, as said below
- merge_weights: float32 [128, 4], P('dp'), may hold values from 0.1 to 1
- owner_slot: int32 [32], replicated, may hold values from 0 to 63, as said below
Outputs:
- layer_out: bfloat16 [32768, 2048], P('dp', 'tensor')
- grad_hidden: bfloat16 [32768, 1408], P('dp', 'tensor')
- expert_grad: float32 [1408, 64, 2048], P('tensor', 'dp')
Inputs may be any that keep to these rules, and one draw needn't show every extreme that they name: `expert_ids`: each segment lists 4 different experts; the 2 segments of one index of dp list exactly 6 different experts together. `owner_slot`: different experts have different slots; slot 63 always holds an expert.
All inputs are finite; a program needn't handle non-finite values.
Results may differ from a plain program's by a relative error of at most 0.013.
Values may be sent and summed in bfloat16 or wider, within the bound.
A program may use at most 128 MiB of HBM per device.

v0:
```python
import jax
import jax.numpy as jnp
from jax import lax
from jax.sharding import PartitionSpec as P

E = 32
K = 4
POOL = 6


def pool_members(id_rows):
    listed = id_rows.reshape(-1)
    experts = jnp.arange(E, dtype=jnp.int32)
    present = jnp.any(listed[None, :] == experts[:, None], axis=1)
    ranking = jnp.cumsum(present.astype(jnp.int32)) - 1
    places = jnp.arange(POOL, dtype=jnp.int32)
    chosen = present[None, :] & (ranking[None, :] == places[:, None])
    return jnp.sum(jnp.where(chosen, experts[None, :], 0), axis=1)


def merge_coefficients(id_rows, weight_rows, targets):
    matches = id_rows[:, :, None] == targets[None, None, :]
    return jnp.sum(jnp.where(matches, weight_rows[:, :, None], 0.0), axis=1)


def body(hidden_act, cotangent, down_table, expert_ids, merge_weights, owner_slot):
    dp_count = lax.axis_size("dp")
    seg_count = expert_ids.shape[0]
    ff_local, slot_local, width = down_table.shape
    stripe = width // dp_count
    row_count = hidden_act.shape[0]
    seg_len = row_count // seg_count
    every_expert = jnp.arange(E, dtype=jnp.int32)
    all_ids, all_weights = (
        lax.all_gather(expert_ids, "dp", axis=0, tiled=True),
        lax.all_gather(merge_weights, "dp", axis=0, tiled=True),
    )
    ids_by_dev = all_ids.reshape(dp_count, seg_count, K)
    weights_by_dev = all_weights.reshape(dp_count, seg_count, K)
    pools_all = jax.vmap(pool_members)(ids_by_dev)
    my_pool = pools_all[lax.axis_index("dp")]
    my_coef = merge_coefficients(expert_ids, merge_weights, my_pool)
    member_table = (pools_all.T[:, :, None] == every_expert[None, None, :]).astype(jnp.bfloat16)
    stripes = lax.all_to_all(down_table, "dp", split_axis=2, concat_axis=1, tiled=True)
    by_expert = jnp.take(stripes, owner_slot, axis=1)
    outgoing = jnp.take(by_expert, pools_all.T, axis=1).reshape(ff_local, POOL, width)
    panel_set = lax.all_to_all(outgoing, "dp", split_axis=2, concat_axis=2, tiled=True)
    merged = jnp.sum(
        panel_set[:, None, :, :].astype(jnp.float32) * my_coef[None, :, :, None], axis=2
    ).astype(jnp.bfloat16)
    hidden_seg = hidden_act.reshape(seg_count, seg_len, ff_local)
    partial_rows = jnp.einsum(
        "stf,fsd->std", hidden_seg, merged, preferred_element_type=jnp.float32
    ).reshape(row_count, width)
    layer_out = lax.psum_scatter(
        partial_rows.astype(jnp.bfloat16), "tensor", scatter_dimension=1, tiled=True
    )
    full_cot = lax.all_gather(cotangent, "tensor", axis=1, tiled=True)
    cot_seg = full_cot.reshape(seg_count, seg_len, width)
    grad_hidden = (
        jnp.einsum("std,fsd->stf", cot_seg, merged, preferred_element_type=jnp.float32)
        .astype(jnp.bfloat16)
        .reshape(row_count, ff_local)
    )
    seg_grads = jnp.einsum(
        "stf,std->fsd", hidden_seg, cot_seg, preferred_element_type=jnp.float32
    ).astype(jnp.bfloat16)
    returned = lax.all_to_all(seg_grads, "dp", split_axis=2, concat_axis=2, tiled=True).reshape(
        ff_local, seg_count, dp_count, stripe
    )
    pool_coef = jax.vmap(merge_coefficients)(ids_by_dev, weights_by_dev, pools_all)
    coef_view = jnp.transpose(pool_coef, (1, 2, 0))
    group_sums = jnp.sum(
        returned[:, :, None, :, :].astype(jnp.float32) * coef_view[None, :, :, :, None], axis=1
    ).astype(jnp.bfloat16)
    grad_stripes = jnp.einsum(
        "fprd,pre->fed", group_sums, member_table, preferred_element_type=jnp.float32
    )
    slotted = (
        jnp.zeros((ff_local, slot_local * dp_count, stripe), jnp.float32)
        .at[:, owner_slot, :]
        .set(grad_stripes)
    )
    expert_grad = lax.all_to_all(
        slotted.astype(jnp.bfloat16), "dp", split_axis=1, concat_axis=2, tiled=True
    ).astype(slotted.dtype)
    return (layer_out, grad_hidden, expert_grad)


def solution(mesh):
    placed = (
        P("dp", "tensor"),
        P("dp", "tensor"),
        P("tensor", "dp", None),
        P("dp", None),
        P("dp", None),
        P(),
    )
    return jax.shard_map(
        body,
        mesh=mesh,
        in_specs=placed,
        out_specs=(P("dp", "tensor"), P("dp", "tensor"), P("tensor", "dp", None)),
        check_vma=False,
    )
```

profile of v0, /device:TPU:1, one launch (start us, length us, event | category | flops | bytes accessed | tf_op | source)
XLA Modules:
  0.0 478.6 jit_solution(9711148216334973201)
XLA Ops:
  7.2 4.5 copy.81
  12.2 11.6 %reduce.2 = bf16[2048,176]{1,0:T(8,128)(2,1)S(1)} reduce(bf16[2048,1,176]{2,1,0:T(2,128)(2,1)S(1)} %bitcast.55, bf16[]{:T(256)} %broadcast.42), dimensions={1}, to_apply=%bitcast.44.reduce_sub_computation | reduce | bytes 1441794
  23.9 2.6 reshape.124
  26.5 11.6 %all-to-all-start = ((bf16[64,2,2816]{2,1,0:T(2,128)(2,1)}), bf16[64,2,2816]{2,1,0:T(2,128)(2,1)S(1)}, u32[]{:S(2)}, u32[]{:S(2)}) async-start(bf16[64,2,2816]{2,1,0:T(2,128)(2,1)} %reshape.124), calls=%async_computation | async-start | bytes 1441792 | tf_op jit(solution)/shard_map/all_to_all | solution.py:44
  38.1 50.6 %all-gather = s32[64,2,4]{2,1,0:T(2,128)S(1)} all-gather(s32[1,2,4]{2,1,0:T(2,128)S(1)} %bitcast.65), channel_id=1, replica_groups=mesh['dp'=64,'tensor'=8] {'dp'}, dimensions={0}, use_global_device_ids=true | all-gather | bytes 2080 | tf_op jit(solution)/shard_map/all_gather | solution.py:35
  89.8 3.2 reshape.125
  93.8 13.3 %gather_fusion.1 = bf16[384,176,32]{1,2,0:T(8,128)(2,1)} fusion(bf16[176,32,32]{0,2,1:T(8,128)(2,1)S(1)} %select_bitcast_fusion, s32[1024]{0:T(1024)S(1)} %pad_clamp_fusion), kind=kCustom, calls=%fused_computation.1 | custom fusion | bytes 8652288 | tf_op jit(solution)/shard_map/jit(_take)/gather | solution.py:46
  107.2 6.2 %broadcast_select_fusion = bf16[176,6,2048]{0,2,1:T(8,128)(2,1)S(1)} fusion(bf16[176,6,2048]{0,2,1:T(8,128)(2,1)} %bitcast.51, pred[6,2048]{1,0:T(8,128)(4,1)S(1)} %broadcast_in_dim.86), kind=kLoop, calls=%fused_computation.7 | loop fusion | flops 2162688 | bytes 8663040 | tf_op jit(solution)/shard_map/jit(_take)/select_n | solution.py:46
  113.4 22.3 %copy.82 = bf16[176,6,2048]{0,1,2:T(8,128)(2,1)} copy(bf16[176,6,2048]{0,2,1:T(8,128)(2,1)S(1)} %broadcast_select_fusion) | data formatting | bytes 8650752 | tf_op jit(solution)/shard_map/jit(_take)/select_n | solution.py:46
  135.7 8.6 %all-to-all-start.1 = ((bf16[176,6,2048]{0,1,2:T(8,128)(2,1)}), bf16[176,6,2048]{0,1,2:T(8,128)(2,1)}, u32[]{:S(2)}, u32[]{:S(2)}) async-start(bf16[176,6,2048]{0,1,2:T(8,128)(2,1)} %copy.82), calls=%async_computation.1 | async-start | bytes 16777216 | tf_op jit(solution)/shard_map/all_to_all | solution.py:47
  145.1 53.0 %all-gather.4.cloned.1.call-done = bf16[512,2048]{1,0:T(8,128)(2,1)} async-done(((bf16[512,256]{1,0:T(8,128)(2,1)}), bf16[512,2048]{1,0:T(8,128)(2,1)}) %all-gather.4.cloned.1.call-update) | async-done | bytes 2097168 | tf_op jit(solution)/shard_map/all_gather | solution.py:58
  198.0 2.1 fusion.2
  200.2 3.8 copy.87
  204.0 122.7 %all-to-all-done.1 = bf16[176,6,2048]{0,1,2:T(8,128)(2,1)} async-done(((bf16[176,6,2048]{0,1,2:T(8,128)(2,1)}), bf16[176,6,2048]{0,1,2:T(8,128)(2,1)}, u32[]{:S(2)}, u32[]{:S(2)}) %all-to-all-start.1) | async-done | bytes 4325408 | tf_op jit(solution)/shard_map/all_to_all | solution.py:47
  326.7 10.1 %all-to-all-start.2 = ((bf16[176,2,2048]{0,1,2:T(2,128)(2,1)}), bf16[176,2,2048]{0,1,2:T(2,128)(2,1)S(1)}, u32[]{:S(2)}, u32[]{:S(2)}) async-start(bf16[176,2,2048]{0,1,2:T(2,128)(2,1)} %copy.87), calls=%async_computation.3 | async-start | bytes 4194304 | tf_op jit(solution)/shard_map/all_to_all | solution.py:68
  337.1 11.3 %copy.83 = bf16[176,6,2048]{2,0,1:T(8,128)(2,1)} copy(bf16[176,6,2048]{0,1,2:T(8,128)(2,1)} %all-to-all-done.1) | data formatting | bytes 8650752 | tf_op jit(solution)/shard_map/all_to_all | solution.py:47
  348.4 6.6 %convert_element_type.68 = f32[176,6,2048]{2,0,1:T(8,128)} convert(bf16[176,6,2048]{2,0,1:T(8,128)(2,1)} %copy.83) | non-fusion elementwise | flops 2162688 | bytes 12976128 | tf_op jit(solution)/shard_map/convert_element_type | solution.py:49
  355.0 4.8 multiply_reduce_fusion.1
  360.9 2.1 convolution_convert_fusion
  363.0 53.9 %all-gather.1 = f32[64,2,4]{2,1,0:T(2,128)S(1)} all-gather(f32[1,2,4]{2,1,0:T(2,128)S(1)} %bitcast.66), channel_id=1, replica_groups=mesh['dp'=64,'tensor'=8] {'dp'}, dimensions={0}, use_global_device_ids=true | all-gather | bytes 2080 | tf_op jit(solution)/shard_map/all_gather | solution.py:36
  417.7 4.2 multiply_reduce_fusion
  421.9 3.7 fusion.3
  428.2 35.5 %all_to_all.31 = bf16[176,64,32]{0,2,1:T(8,128)(2,1)S(1)} all-to-all(bf16[176,64,32]{0,2,1:T(8,128)(2,1)S(1)} %convert_element_type.80), channel_id=1, replica_groups=mesh['dp'=64,'tensor'=8] {'dp'}, dimensions={1} | all-to-all | bytes 1441792 | tf_op jit(solution)/shard_map/all_to_all | solution.py:84
  465.2 5.1 %copy.93 = f32[176,1,2048]{2,1,0:T(1,128)} copy(f32[176,1,2048]{0,2,1:T(8,128)} %bitcast_convert_fusion) | data formatting | bytes 2883584
  (54 shorter events, 10.8 us)
Async XLA Ops:
  23.9 14.3 %copy-start.4 = (s32[2,4]{1,0:T(2,128)S(1)}, s32[2,4]{1,0:T(2,128)}, u32[]{:S(2)}) copy-start(s32[2,4]{1,0:T(2,128)} %param.9) | copy-start | bytes 100
  23.9 65.9 %copy-start.6 = (s32[32]{0:T(128)S(1)}, s32[32]{0:T(128)}, u32[]{:S(2)}) copy-start(s32[32]{0:T(128)} %param.11) | copy-start | bytes 388
  26.5 63.3 %all-to-all-start = ((bf16[64,2,2816]{2,1,0:T(2,128)(2,1)}), bf16[64,2,2816]{2,1,0:T(2,128)(2,1)S(1)}, u32[]{:S(2)}, u32[]{:S(2)}) async-start(bf16[64,2,2816]{2,1,0:T(2,128)(2,1)} %reshape.124), calls=%async_computation | async-start | bytes 1441792 | tf_op jit(solution)/shard_map/all_to_all | solution.py:44
  135.7 62.3 %copy-start.3 = (bf16[512,176]{0,1:T(8,128)(2,1)S(1)}, bf16[512,176]{0,1:T(8,128)(2,1)}, u32[]{:S(2)}) copy-start(bf16[512,176]{0,1:T(8,128)(2,1)} %param.6) | copy-start | bytes 540676
  135.7 191.0 %all-to-all-start.1 = ((bf16[176,6,2048]{0,1,2:T(8,128)(2,1)}), bf16[176,6,2048]{0,1,2:T(8,128)(2,1)}, u32[]{:S(2)}, u32[]{:S(2)}) async-start(bf16[176,6,2048]{0,1,2:T(8,128)(2,1)} %copy.82), calls=%async_computation.1 | async-start | bytes 16777216 | tf_op jit(solution)/shard_map/all_to_all | solution.py:47
  144.3 53.7 %all-gather.4.cloned.1.call-start = ((), (), s32[]{:S(2)}) async-start(), calls=%async_computation.6 | async-start | bytes 2359296 | tf_op jit(solution)/shard_map/all_gather | solution.py:58
  204.0 133.0 %copy-start.5 = (f32[2,4]{1,0:T(2,128)S(1)}, f32[2,4]{1,0:T(2,128)}, u32[]{:S(2)}) copy-start(f32[2,4]{1,0:T(2,128)} %param.10) | copy-start | bytes 100
  326.7 90.3 %all-to-all-start.2 = ((bf16[176,2,2048]{0,1,2:T(2,128)(2,1)}), bf16[176,2,2048]{0,1,2:T(2,128)(2,1)S(1)}, u32[]{:S(2)}, u32[]{:S(2)}) async-start(bf16[176,2,2048]{0,1,2:T(2,128)(2,1)} %copy.87), calls=%async_computation.3 | async-start | bytes 4194304 | tf_op jit(solution)/shard_map/all_to_all | solution.py:68
  336.8 135.0 %reduce-scatter.2.cloned.1.call-start = ((), (), s32[]{:S(2)}) async-start(), calls=%async_computation.5 | async-start | bytes 2359296 | tf_op jit(solution)/shard_map/reduce_scatter | solution.py:55
  359.8 1.1 copy-start
  465.2 5.1 %copy-start.1 = (bf16[176,2,2048]{2,0,1:T(8,128)(2,1)S(1)}, bf16[176,2,2048]{2,0,1:T(8,128)(2,1)}, u32[]{:S(2)}) copy-start(bf16[176,2,2048]{2,0,1:T(8,128)(2,1)} %copy-done) | copy-start | bytes 4325380
  465.2 5.1 %copy-start.2 = (bf16[512,2048]{1,0:T(8,128)(2,1)S(1)}, bf16[512,2048]{1,0:T(8,128)(2,1)}, u32[]{:S(2)}) copy-start(bf16[512,2048]{1,0:T(8,128)(2,1)} %all-gather.4.cloned.1.call-done) | copy-start | bytes 6291460
Sparse Core Ops, SparseCore 0:
  147.2 50.8 all-gather.3
  363.1 45.3 reduce-scatter.1
where the time goes:
time: 480 us; the launch traced here: 479 us
  waiting for transfers between devices  176 us (37%)
  blocking collectives  140 us (29%)
  local copies, waits for them, and re-layouts  72.6 us (15%)
  other arithmetic  36.2 us (8%)
  starting transfers between devices  30.4 us (6%)
  between operations  14.3 us (3%)
  matrix products  8.77 us (2%)
    all_to_all x1, waiting for transfers between devices, body(): lax.all_to_all(outgoing, 'dp', split_axis=2, concat_axis=2, tiled=True)  123 us
    all_gather x1, blocking collectives, body(): lax.all_gather(merge_weights, 'dp', axis=0, tiled=True)  53.9 us
    all_gather x1, waiting for transfers between devices, body(): full_cot = lax.all_gather(cotangent, 'tensor', axis=1, tiled=True)  53 us
    all_gather x1, blocking collectives, body(): lax.all_gather(expert_ids, 'dp', axis=0, tiled=True)  50.6 us
    all_to_all x1, blocking collectives, body(): lax.all_to_all(slotted.astype(jnp.bfloat16), 'dp', split_axis=1, concat_a...  35.5 us
    select_n x1, local copies, waits for them, and re-layouts, body(): jnp.take(by_expert, pools_all.T, axis=1).reshape(ff_local, POOL, width)  22.3 us
    unnamed x20, local copies, waits for them, and re-layouts  17.2 us
    gather x1, local copies, waits for them, and re-layouts, body(): jnp.take(by_expert, pools_all.T, axis=1).reshape(ff_local, POOL, width)  13.3 us
  transfers between devices with their start and end apart: 5, of which 2 were waited for; matrix products, arithmetic and copies ran while one was open for 11% of the time, Pallas kernels for 0%

commit v1 on v0

--- a/solution.py
+++ b/solution.py
@@ -41,7 +41,10 @@
     my_pool = pools_all[lax.axis_index("dp")]
     my_coef = merge_coefficients(expert_ids, merge_weights, my_pool)
     member_table = (pools_all.T[:, :, None] == every_expert[None, None, :]).astype(jnp.bfloat16)
-    stripes = lax.all_to_all(down_table, "dp", split_axis=2, concat_axis=1, tiled=True)
+    stripes = jnp.concatenate(
+        lax.all_to_all(jnp.stack(jnp.split(down_table, lax.axis_size("dp"), axis=2)), "dp", 0, 0),
+        axis=1,
+    )
     by_expert = jnp.take(stripes, owner_slot, axis=1)
     outgoing = jnp.take(by_expert, pools_all.T, axis=1).reshape(ff_local, POOL, width)
     panel_set = lax.all_to_all(outgoing, "dp", split_axis=2, concat_axis=2, tiled=True)

time: 480 us -> 514 us (1.071)
  local copies, waits for them, and re-layouts: 72.6 us -> 112 us
  other arithmetic: 36.2 us -> 24.6 us
  blocking collectives: 140 us -> 147 us
    unnamed x20 -> x144, local copies, waits for them, and re-layouts: 17.2 us -> 51.7 us
    unnamed x1 -> x0, other arithmetic: 11.6 us -> none
    all_gather x1, blocking collectives: 50.6 us -> 57.6 us  [body(): lax.all_gather(expert_ids, 'dp', axis=0, tiled=True)]
  transfers between devices with their start and end apart: 5 -> 5, of which waited for: 2 -> 2; matrix products, arithmetic and copies ran while one was open for 11% -> 10% of each run, Pallas kernels for 0% -> 0%
where the time goes in v1:
time: 514 us; the launch traced here: 513 us
  waiting for transfers between devices  176 us (34%)
  blocking collectives  147 us (29%)
  local copies, waits for them, and re-layouts  112 us (22%)
  starting transfers between devices  30.1 us (6%)
  other arithmetic  24.6 us (5%)
  between operations  14.4 us (3%)
  matrix products  8.77 us (2%)
    all_to_all x1, waiting for transfers between devices, body(): lax.all_to_all(outgoing, 'dp', split_axis=2, concat_axis=2, tiled=True)  123 us
    all_gather x1, blocking collectives, body(): lax.all_gather(expert_ids, 'dp', axis=0, tiled=True)  57.6 us
    all_gather x1, blocking collectives, body(): lax.all_gather(merge_weights, 'dp', axis=0, tiled=True)  53.9 us
    all_gather x1, waiting for transfers between devices, body(): full_cot = lax.all_gather(cotangent, 'tensor', axis=1, tiled=True)  53 us
    unnamed x144, local copies, waits for them, and re-layouts  51.7 us
    all_to_all x1, blocking collectives, body(): lax.all_to_all(slotted.astype(jnp.bfloat16), 'dp', split_axis=1, concat_a...  35.5 us
    select_n x1, local copies, waits for them, and re-layouts, body(): jnp.take(by_expert, pools_all.T, axis=1).reshape(ff_local, POOL, width)  22.3 us
    gather x1, local copies, waits for them, and re-layouts, body(): jnp.take(by_expert, pools_all.T, axis=1).reshape(ff_local, POOL, width)  13.3 us
  transfers between devices with their start and end apart: 5, of which 2 were waited for; matrix products, arithmetic and copies ran while one was open for 10% of the time, Pallas kernels for 0%

profile of v1, /device:TPU:1, one launch (start us, length us, event | category | flops | bytes accessed | tf_op | source)
XLA Modules:
  0.0 512.8 jit_solution(2143279396814339660)
XLA Ops:
  7.2 1.2 fusion.21
  8.3 2.2 fusion.20
  57.0 11.6 %all-to-all-start = ((bf16[64,176,1,32]{1,3,2,0:T(8,128)(2,1)}), bf16[64,176,1,32]{1,3,2,0:T(8,128)(2,1)S(1)}, u32[]{:S(2)}, u32[]{:S(2)}) async-start(bf16[64,176,1,32]{1,3,2,0:T(8,128)(2,1)} %constant_dynamic-update-slice_fusion), calls=%async_computation | async-start | bytes 2097152 | tf_op jit(solution)/shard_map/all_to_all | solution.py:45
  68.7 57.6 %all-gather = s32[64,2,4]{2,1,0:T(2,128)S(1)} all-gather(s32[1,2,4]{2,1,0:T(2,128)S(1)} %bitcast.191), channel_id=1, replica_groups=mesh['dp'=64,'tensor'=8] {'dp'}, dimensions={0}, use_global_device_ids=true | all-gather | bytes 2080 | tf_op jit(solution)/shard_map/all_gather | solution.py:35
  128.1 13.3 %gather_fusion.1 = bf16[384,176,32]{1,2,0:T(8,128)(2,1)} fusion(bf16[176,32,32]{0,2,1:T(8,128)(2,1)S(1)} %select_bitcast_fusion, s32[1024]{0:T(1024)S(1)} %pad_clamp_fusion), kind=kCustom, calls=%fused_computation.1 | custom fusion | bytes 8652288 | tf_op jit(solution)/shard_map/jit(_take)/gather | solution.py:49
  141.4 6.2 %broadcast_select_fusion = bf16[176,6,2048]{0,2,1:T(8,128)(2,1)S(1)} fusion(bf16[176,6,2048]{0,2,1:T(8,128)(2,1)} %bitcast.179, pred[6,2048]{1,0:T(8,128)(4,1)S(1)} %broadcast_in_dim.86), kind=kLoop, calls=%fused_computation.7 | loop fusion | flops 2162688 | bytes 8663040 | tf_op jit(solution)/shard_map/jit(_take)/select_n | solution.py:49
  147.6 22.3 %copy.334 = bf16[176,6,2048]{0,1,2:T(8,128)(2,1)} copy(bf16[176,6,2048]{0,2,1:T(8,128)(2,1)S(1)} %broadcast_select_fusion) | data formatting | bytes 8650752 | tf_op jit(solution)/shard_map/jit(_take)/select_n | solution.py:49
  169.9 8.3 %all-to-all-start.1 = ((bf16[176,6,2048]{0,1,2:T(8,128)(2,1)}), bf16[176,6,2048]{0,1,2:T(8,128)(2,1)}, u32[]{:S(2)}, u32[]{:S(2)}) async-start(bf16[176,6,2048]{0,1,2:T(8,128)(2,1)} %copy.334), calls=%async_computation.1 | async-start | bytes 16777216 | tf_op jit(solution)/shard_map/all_to_all | solution.py:50
  179.0 53.0 %all-gather.4.cloned.1.call-done = bf16[512,2048]{1,0:T(8,128)(2,1)} async-done(((bf16[512,256]{1,0:T(8,128)(2,1)}), bf16[512,2048]{1,0:T(8,128)(2,1)}) %all-gather.4.cloned.1.call-update) | async-done | bytes 2097168 | tf_op jit(solution)/shard_map/all_gather | solution.py:61
  232.0 2.1 fusion.2
  234.1 3.8 copy.339
  237.9 122.7 %all-to-all-done.1 = bf16[176,6,2048]{0,1,2:T(8,128)(2,1)} async-done(((bf16[176,6,2048]{0,1,2:T(8,128)(2,1)}), bf16[176,6,2048]{0,1,2:T(8,128)(2,1)}, u32[]{:S(2)}, u32[]{:S(2)}) %all-to-all-start.1) | async-done | bytes 4325408 | tf_op jit(solution)/shard_map/all_to_all | solution.py:50
  360.6 10.1 %all-to-all-start.2 = ((bf16[176,2,2048]{0,1,2:T(2,128)(2,1)}), bf16[176,2,2048]{0,1,2:T(2,128)(2,1)S(1)}, u32[]{:S(2)}, u32[]{:S(2)}) async-start(bf16[176,2,2048]{0,1,2:T(2,128)(2,1)} %copy.339), calls=%async_computation.3 | async-start | bytes 4194304 | tf_op jit(solution)/shard_map/all_to_all | solution.py:71
  371.0 11.3 %copy.335 = bf16[176,6,2048]{2,0,1:T(8,128)(2,1)} copy(bf16[176,6,2048]{0,1,2:T(8,128)(2,1)} %all-to-all-done.1) | data formatting | bytes 8650752 | tf_op jit(solution)/shard_map/all_to_all | solution.py:50
  382.3 6.6 %convert_element_type.68 = f32[176,6,2048]{2,0,1:T(8,128)} convert(bf16[176,6,2048]{2,0,1:T(8,128)(2,1)} %copy.335) | non-fusion elementwise | flops 2162688 | bytes 12976128 | tf_op jit(solution)/shard_map/convert_element_type | solution.py:52
  388.9 4.8 multiply_reduce_fusion.1
  394.8 2.1 convolution_convert_fusion
  397.0 53.9 %all-gather.1 = f32[64,2,4]{2,1,0:T(2,128)S(1)} all-gather(f32[1,2,4]{2,1,0:T(2,128)S(1)} %bitcast.192), channel_id=1, replica_groups=mesh['dp'=64,'tensor'=8] {'dp'}, dimensions={0}, use_global_device_ids=true | all-gather | bytes 2080 | tf_op jit(solution)/shard_map/all_gather | solution.py:36
  451.6 4.2 multiply_reduce_fusion
  455.8 3.7 fusion.3
  460.4 1.6 scatter_fusion
  462.1 35.5 %all_to_all.24 = bf16[176,64,32]{0,2,1:T(8,128)(2,1)S(1)} all-to-all(bf16[176,64,32]{0,2,1:T(8,128)(2,1)S(1)} %convert_element_type.80), channel_id=1, replica_groups=mesh['dp'=64,'tensor'=8] {'dp'}, dimensions={1} | all-to-all | bytes 1441792 | tf_op jit(solution)/shard_map/all_to_all | solution.py:87
  497.7 1.5 bitcast_convert_fusion
  499.1 5.3 %copy.345 = f32[176,1,2048]{2,1,0:T(1,128)} copy(f32[176,1,2048]{0,2,1:T(8,128)} %bitcast_convert_fusion) | data formatting | bytes 2883584
  (182 shorter events, 53.5 us)
Async XLA Ops:
  7.2 3.4 copy-start.2
  16.6 52.1 %copy-start.5 = (s32[2,4]{1,0:T(2,128)S(1)}, s32[2,4]{1,0:T(2,128)}, u32[]{:S(2)}) copy-start(s32[2,4]{1,0:T(2,128)} %param.9) | copy-start | bytes 100
  17.3 110.0 %copy-start.7 = (s32[32]{0:T(128)S(1)}, s32[32]{0:T(128)}, u32[]{:S(2)}) copy-start(s32[32]{0:T(128)} %param.11) | copy-start | bytes 388
  57.0 70.3 %all-to-all-start = ((bf16[64,176,1,32]{1,3,2,0:T(8,128)(2,1)}), bf16[64,176,1,32]{1,3,2,0:T(8,128)(2,1)S(1)}, u32[]{:S(2)}, u32[]{:S(2)}) async-start(bf16[64,176,1,32]{1,3,2,0:T(8,128)(2,1)} %constant_dynamic-update-slice_fusion), calls=%async_computation | async-start | bytes 2097152 | tf_op jit(solution)/shard_map/all_to_all | solution.py:45
  169.9 62.0 %copy-start.4 = (bf16[512,176]{0,1:T(8,128)(2,1)S(1)}, bf16[512,176]{0,1:T(8,128)(2,1)}, u32[]{:S(2)}) copy-start(bf16[512,176]{0,1:T(8,128)(2,1)} %param.6) | copy-start | bytes 540676
  169.9 190.7 %all-to-all-start.1 = ((bf16[176,6,2048]{0,1,2:T(8,128)(2,1)}), bf16[176,6,2048]{0,1,2:T(8,128)(2,1)}, u32[]{:S(2)}, u32[]{:S(2)}) async-start(bf16[176,6,2048]{0,1,2:T(8,128)(2,1)} %copy.334), calls=%async_computation.1 | async-start | bytes 16777216 | tf_op jit(solution)/shard_map/all_to_all | solution.py:50
  178.3 53.7 %all-gather.4.cloned.1.call-start = ((), (), s32[]{:S(2)}) async-start(), calls=%async_computation.6 | async-start | bytes 2359296 | tf_op jit(solution)/shard_map/all_gather | solution.py:61
  237.9 133.0 %copy-start.6 = (f32[2,4]{1,0:T(2,128)S(1)}, f32[2,4]{1,0:T(2,128)}, u32[]{:S(2)}) copy-start(f32[2,4]{1,0:T(2,128)} %param.10) | copy-start | bytes 100
  360.6 90.3 %all-to-all-start.2 = ((bf16[176,2,2048]{0,1,2:T(2,128)(2,1)}), bf16[176,2,2048]{0,1,2:T(2,128)(2,1)S(1)}, u32[]{:S(2)}, u32[]{:S(2)}) async-start(bf16[176,2,2048]{0,1,2:T(2,128)(2,1)} %copy.339), calls=%async_computation.3 | async-start | bytes 4194304 | tf_op jit(solution)/shard_map/all_to_all | solution.py:71
  370.7 135.2 %reduce-scatter.2.cloned.1.call-start = ((), (), s32[]{:S(2)}) async-start(), calls=%async_computation.5 | async-start | bytes 2359296 | tf_op jit(solution)/shard_map/reduce_scatter | solution.py:58
  393.7 1.1 copy-start
  497.6 6.7 %copy-start.1 = (bf16[176,2,2048]{2,0,1:T(8,128)(2,1)S(1)}, bf16[176,2,2048]{2,0,1:T(8,128)(2,1)}, u32[]{:S(2)}) copy-start(bf16[176,2,2048]{2,0,1:T(8,128)(2,1)} %copy-done) | copy-start | bytes 4325380
  497.6 6.7 %copy-start.3 = (bf16[512,2048]{1,0:T(8,128)(2,1)S(1)}, bf16[512,2048]{1,0:T(8,128)(2,1)}, u32[]{:S(2)}) copy-start(bf16[512,2048]{1,0:T(8,128)(2,1)} %all-gather.4.cloned.1.call-done) | copy-start | bytes 6291460
Sparse Core Ops, SparseCore 0:
  181.1 50.8 all-gather.3
  397.1 45.3 reduce-scatter.1
